TPU v7x, 128 devices: a whole 4x4x4 slice. The times are simulated.
128 devices in a mesh: brick: 8 (over y, core), grp: 16 (over x, z).
Axes of the slice: x: 4, y: 4, z: 4, core: 2. Of those that a mesh axis runs over, the one named last changes fastest.
Arguments:
- source: float32 [16, 8, 2, 32, 1024], P('grp', 'brick'), may hold values from -21 to 21
- uptake: float32 [16, 8, 2, 32, 1024], P('grp', 'brick'), may hold values from 0.00015 to 0.006
- conductance: float32 [16, 8, 6, 2, 32, 1024], P('grp', 'brick'), may hold values from 0 to 3, as said below
- occupancy: int32 [16, 2, 8], replicated, may hold values from 0 to 1, as said below
- assignment: int32 [8], replicated, may hold values from 0 to 7, as said below
Outputs:
- solution_field: float32 [16, 8, 2, 32, 1024], P('grp', 'brick')
- residual: float32 [16, 8, 2, 32, 1024], P('grp', 'brick')
Inputs may be any that keep to these rules, and one draw needn't show every extreme that they name: `occupancy`: 1 marks an occupied brick; in every draw one patch of some slab has all its bricks occupied. `assignment`: each patch is held by exactly one index of brick. `conductance`: equal at both ends of a bond: the value toward +x at a cell is the value toward -x at its +x neighbour, likewise for y and z, the lattice being read cyclically; values toward +z and -z are 0.3 or more.
All inputs are finite; a program needn't handle non-finite values.
Results may differ from a plain program's by a relative error of at most 0.0003.
Values sent between devices are 32-bit elements; how exact they have to be, the bound alone decides.
A program may use at most 128 MiB of HBM per device.

v0:
```python
import jax
import jax.numpy as jnp
from jax import lax
from jax.sharding import PartitionSpec as P

BS = 32
PATCH_X = 1
PATCH_Y = 2
ITERS = 3
OMEGA = 0.6


def extended_2(block, sides, width):
    for axis, dim in sides:
        count = lax.axis_size(axis)
        forward = [(i, i + 1) for i in range(count - 1)]
        backward = [(target, source) for source, target in forward]
        low = lax.ppermute(
            lax.slice_in_dim(block, block.shape[dim] - width, None, axis=dim), axis, forward
        )
        high = lax.ppermute(lax.slice_in_dim(block, 0, width, axis=dim), axis, backward)
        block = jnp.concatenate([low, block, high], axis=dim)
    return block


def assemble(coarse_diag, couplings, strides):
    extent = coarse_diag.shape[0]
    matrix = jnp.diag(coarse_diag)
    for coupling, stride in zip(couplings, strides):
        banded = coupling[: extent - stride]
        matrix = matrix - jnp.diag(banded, stride) - jnp.diag(banded, -stride)
    return matrix


def pad_rows(block, capacity):
    return jnp.pad(block, ((0, capacity - block.shape[0]), (0, 0)))


def on_device(source, uptake, conductance, occupancy, assignment):
    face_size = BS * BS
    capacity = max(PATCH_X, PATCH_Y)
    slot_count = PATCH_X * PATCH_Y
    slab_index = lax.axis_index("grp")
    brick_index = lax.axis_index("brick")
    brick_count = lax.axis_size("brick")
    across = brick_count // 2
    peer_ids = jnp.arange(brick_count, dtype=jnp.int32)
    patch_index = assignment[brick_index]
    patch_row = patch_index // across
    patch_column = patch_index % across

    def owner_of(row_shift, column_shift):
        row_target = patch_row + row_shift
        column_target = patch_column + column_shift
        inside = (
            (row_target >= 0) & (row_target < 2) & (column_target >= 0) & (column_target < across)
        )
        holder = jnp.sum(jnp.where(assignment == row_target * across + column_target, peer_ids, 0))
        return jnp.where(inside, holder, -1)

    wanted = jnp.stack([owner_of(1, 0), owner_of(-1, 0), owner_of(0, 1), owner_of(0, -1)])
    padded = jnp.pad(occupancy, 1)
    window = lax.dynamic_slice(
        padded,
        (slab_index, patch_row * PATCH_X, patch_column * PATCH_Y),
        (3, PATCH_X + 2, PATCH_Y + 2),
    ).astype(jnp.float32)
    centre = window[1, 1:-1, 1:-1].reshape(slot_count)
    toward = [
        window[1, 2:, 1:-1],
        window[1, :-2, 1:-1],
        window[1, 1:-1, 2:],
        window[1, 1:-1, :-2],
        window[2, 1:-1, 1:-1],
        window[0, 1:-1, 1:-1],
    ]
    first_axis = lax.broadcasted_iota(jnp.int32, (1, BS, face_size), 1)
    flat_axis = lax.broadcasted_iota(jnp.int32, (1, BS, face_size), 2)
    second_axis = flat_axis // BS
    third_axis = flat_axis % BS
    cube_third = lax.broadcasted_iota(jnp.int32, (1, BS, BS, BS), 3)
    borders = [
        first_axis == BS - 1,
        first_axis == 0,
        second_axis == BS - 1,
        second_axis == 0,
        third_axis == BS - 1,
        third_axis == 0,
    ]
    bonds = conductance[0, 0]
    live_here = centre[:, None, None]
    effective = []
    for direction in range(6):
        neighbour_live = toward[direction].reshape(slot_count)[:, None, None]
        active = jnp.where(borders[direction], live_here * neighbour_live, live_here)
        effective.append(bonds[direction] * active)
    absorb = uptake[0, 0]
    diagonal = absorb
    for direction in range(6):
        diagonal = diagonal + effective[direction]

    def apply_operator(field):
        lower_x = field[:, 0, :]
        upper_x = field[:, BS - 1, :]
        lower_y = field[:, :, :BS].reshape(slot_count, face_size)
        upper_y = field[:, :, face_size - BS :].reshape(slot_count, face_size)
        cube = field.reshape(slot_count, BS, BS, BS)
        lower_z = cube[:, :, :, 0].reshape(slot_count, face_size)
        upper_z = cube[:, :, :, BS - 1].reshape(slot_count, face_size)
        grid_lower_x = lower_x.reshape(PATCH_X, PATCH_Y, face_size)
        grid_upper_x = upper_x.reshape(PATCH_X, PATCH_Y, face_size)
        grid_lower_y = lower_y.reshape(PATCH_X, PATCH_Y, face_size)
        grid_upper_y = upper_y.reshape(PATCH_X, PATCH_Y, face_size)
        outgoing_sides = jnp.stack(
            [
                pad_rows(grid_lower_x[0], capacity),
                pad_rows(grid_upper_x[PATCH_X - 1], capacity),
                pad_rows(grid_lower_y[:, 0], capacity),
                pad_rows(grid_upper_y[:, PATCH_Y - 1], capacity),
            ]
        )
        portion = lax.all_gather(outgoing_sides[None], "brick", axis=0, tiled=True)
        sources = jnp.arange(portion.shape[0], dtype=jnp.int32)
        matches = sources[:, None] == wanted[None, :]
        remote = jnp.zeros((4, capacity, face_size), jnp.float32) + jnp.sum(
            jnp.where(matches[:, :, None, None], portion, 0.0), axis=0
        )
        stacked = jnp.stack([lower_z, upper_z])
        extended = extended_2(stacked, (("grp", 0),), 1)
        from_below = extended[0].reshape(slot_count, BS, BS, 1)
        from_above = extended[3].reshape(slot_count, BS, BS, 1)
        beyond_xplus = jnp.concatenate(
            [grid_lower_x[1:], remote[0, :PATCH_Y][None]], axis=0
        ).reshape(slot_count, face_size)
        beyond_xminus = jnp.concatenate(
            [remote[1, :PATCH_Y][None], grid_upper_x[:-1]], axis=0
        ).reshape(slot_count, face_size)
        beyond_yplus = jnp.concatenate(
            [grid_lower_y[:, 1:], remote[2, :PATCH_X][:, None]], axis=1
        ).reshape(slot_count, BS, BS)
        beyond_yminus = jnp.concatenate(
            [remote[3, :PATCH_X][:, None], grid_upper_y[:, :-1]], axis=1
        ).reshape(slot_count, BS, BS)
        upper_neighbour = jnp.where(
            cube_third == BS - 1, from_above, jnp.roll(cube, -1, axis=3)
        ).reshape(slot_count, BS, face_size)
        lower_neighbour = jnp.where(cube_third == 0, from_below, jnp.roll(cube, 1, axis=3)).reshape(
            slot_count, BS, face_size
        )
        total = diagonal * field
        total = total - effective[0] * jnp.concatenate(
            [field[:, 1:, :], beyond_xplus[:, None, :]], axis=1
        )
        total = total - effective[1] * jnp.concatenate(
            [beyond_xminus[:, None, :], field[:, :-1, :]], axis=1
        )
        total = total - effective[2] * jnp.concatenate([field[:, :, BS:], beyond_yplus], axis=2)
        total = total - effective[3] * jnp.concatenate(
            [beyond_yminus, field[:, :, : face_size - BS]], axis=2
        )
        total = total - effective[4] * upper_neighbour
        total = total - effective[5] * lower_neighbour
        return total

    slot_ids = jnp.arange(slot_count)
    brick_first = slot_ids // PATCH_Y
    brick_second = slot_ids % PATCH_Y
    inside = [
        (brick_first < PATCH_X - 1).astype(jnp.float32),
        (brick_first > 0).astype(jnp.float32),
        (brick_second < PATCH_Y - 1).astype(jnp.float32),
        (brick_second > 0).astype(jnp.float32),
    ]
    face_sums = [
        jnp.sum(effective[0][:, BS - 1, :], axis=1),
        jnp.sum(effective[1][:, 0, :], axis=1),
        jnp.sum(effective[2][:, :, face_size - BS :], axis=(1, 2)),
        jnp.sum(effective[3][:, :, :BS], axis=(1, 2)),
        jnp.sum(effective[4].reshape(slot_count, BS, BS, BS)[:, :, :, BS - 1], axis=(1, 2)),
        jnp.sum(effective[5].reshape(slot_count, BS, BS, BS)[:, :, :, 0], axis=(1, 2)),
    ]
    coarse_diag = jnp.sum(absorb, axis=(1, 2))
    for direction in range(4):
        coarse_diag = coarse_diag + face_sums[direction] * inside[direction]
    coarse_diag = coarse_diag + face_sums[4] + face_sums[5]
    record = jnp.stack(
        [coarse_diag, face_sums[0] * inside[0], face_sums[2] * inside[2], face_sums[4]]
    )[None]
    gathered = lax.all_gather(record, "grp", axis=0, tiled=True)
    columns = jnp.transpose(gathered, (1, 0, 2)).reshape(4, -1)
    matrix = assemble(columns[0], (columns[1], columns[2], columns[3]), (PATCH_Y, 1, slot_count))
    factor = jnp.linalg.cholesky(matrix)

    def coarse_solve(residual_field):
        totals = jnp.sum(residual_field, axis=(1, 2))
        gathered_terms = lax.all_gather(totals[None], "grp", axis=0, tiled=True).reshape(-1, 1)
        middle = lax.linalg.triangular_solve(factor, gathered_terms, left_side=True, lower=True)
        result = lax.linalg.triangular_solve(
            factor, middle, left_side=True, lower=True, transpose_a=True
        )
        return lax.dynamic_slice_in_dim(result[:, 0], slab_index * slot_count, slot_count)

    def precondition(residual_field):
        smoothed = OMEGA * residual_field / diagonal
        smoothed = smoothed + OMEGA * (residual_field - apply_operator(smoothed)) / diagonal
        return smoothed + coarse_solve(residual_field)[:, None, None]

    forcing = source[0, 0] * live_here
    solution_field = jnp.zeros_like(forcing)
    residual = forcing

    def global_sum(values):
        return lax.psum(jnp.sum(values), ("brick", "grp"))

    search = precondition(residual)
    energy = global_sum(residual * search)
    for iteration in range(ITERS):
        mapped = apply_operator(search)
        step_size = energy / global_sum(search * mapped)
        solution_field = solution_field + step_size * search
        residual = residual - step_size * mapped
        if iteration + 1 < ITERS:
            smoothed = precondition(residual)
            renewed = global_sum(residual * smoothed)
            search = smoothed + renewed / energy * search
            energy = renewed
    return (solution_field[None, None], residual[None, None])


def solution(mesh):
    return jax.shard_map(
        on_device,
        mesh=mesh,
        in_specs=(
            P("grp", "brick", None, None, None),
            P("grp", "brick", None, None, None),
            P("grp", "brick", None, None, None, None),
            P(),
            P(),
        ),
        out_specs=(P("grp", "brick", None, None, None), P("grp", "brick", None, None, None)),
        check_vma=False,
    )
```

profile of v0, /device:TPU:1, one launch (start us, length us, event | category | flops | bytes accessed | tf_op | source)
XLA Modules:
  0.0 1063.9 jit_solution(14409875242148923339)
XLA Ops:
  15.4 2.4 squeeze.120
  22.2 5.7 multiply_divide_fusion.2
  30.5 4.9 collective-permute-start.1
  45.7 14.1 %all-gather = f32[32,2,1024]{2,1,0:T(2,128)S(1)} all-gather(f32[4,2,1024]{2,1,0:T(2,128)S(1)} %copy.294), channel_id=2, replica_groups=mesh['brick'=8,'grp'=16] {'brick'}, dimensions={0}, use_global_device_ids=true | all-gather | bytes 294912 | tf_op jit(solution)/shard_map/all_gather | solution.py:122
  68.6 19.9 %all-gather.10 = f32[16,4,2]{1,2,0:T(2,128)S(1)} all-gather(f32[1,4,2]{1,2,0:T(2,128)S(1)} %bitcast.616), channel_id=3, replica_groups=mesh['brick'=8,'grp'=16] {'grp'}, dimensions={0}, use_global_device_ids=true | all-gather | bytes 544 | tf_op jit(solution)/shard_map/all_gather | solution.py:189
  94.2 31.1 %all-reduce.18 = f32[32]{0:T(128)S(1)} all-reduce(f32[32]{0:T(128)S(1)} %dynamic-update-slice.3), channel_id=4, replica_groups=mesh['brick'=8,'grp'=16] {'grp'}, use_global_device_ids=true, to_apply=%add.18 | all-reduce | flops 32 | bytes 256 | tf_op jit(solution)/shard_map/triangular_solve/reshape.87 | solution.py:197
  130.3 2.9 cholesky.19
  134.6 2.4 custom-call.14
  153.2 8.4 fusion.46
  167.8 2.4 broadcast_in_dim.696
  171.5 2.4 broadcast_in_dim.702
  184.6 25.6 %all-gather.3 = f32[32,2,1024]{2,1,0:T(2,128)S(1)} all-gather(f32[4,2,1024]{2,1,0:T(2,128)S(1)} %copy.298), channel_id=5, replica_groups=mesh['brick'=8,'grp'=16] {'brick'}, dimensions={0}, use_global_device_ids=true | all-gather | bytes 294912 | tf_op jit(solution)/shard_map/all_gather | solution.py:122
  226.1 3.0 pad_maximum_fusion.2
  231.1 2.4 concatenate.676
  233.6 2.4 concatenate.677
  282.5 3.7 multiply_reduce_fusion.3
  286.2 64.0 %all-reduce.21 = (f32[]{:T(128)}, f32[]{:T(128)}) all-reduce(f32[]{:T(128)} %get-tuple-element.21, f32[]{:T(128)} %get-tuple-element.20), channel_id=1, replica_groups=mesh['brick'=8,'grp'=16] {'brick','grp'}, use_global_device_ids=true, to_apply=%region_16.19 | all-reduce | flops 2 | bytes 16 | tf_op jit(solution)/shard_map/psum | solution.py:213
  362.0 13.5 %all-gather.4 = f32[32,2,1024]{2,1,0:T(2,128)S(1)} all-gather(f32[4,2,1024]{2,1,0:T(2,128)S(1)} %copy.304), channel_id=6, replica_groups=mesh['brick'=8,'grp'=16] {'brick'}, dimensions={0}, use_global_device_ids=true | all-gather | bytes 294912 | tf_op jit(solution)/shard_map/all_gather | solution.py:122
  385.3 9.1 multiply_divide_fusion.1
  400.2 31.6 %all-reduce.19 = f32[32]{0:T(128)} all-reduce(f32[32]{0:T(128)} %dynamic-update-slice.4), channel_id=7, replica_groups=mesh['brick'=8,'grp'=16] {'grp'}, use_global_device_ids=true, to_apply=%add.19 | all-reduce | flops 32 | bytes 256 | tf_op jit(solution)/shard_map/triangular_solve/reshape.87 | solution.py:197
  442.0 3.0 pad_maximum_fusion.4
  447.3 3.0 fusion.96
  487.2 3.7 multiply_reduce_fusion.2
  490.9 71.1 %psum.44 = f32[]{:T(128)} all-reduce(f32[]{:T(128)} %get-tuple-element.54), channel_id=1, replica_groups=mesh['brick'=8,'grp'=16] {'brick','grp'}, use_global_device_ids=true, to_apply=%region_23.26 | all-reduce | flops 1 | bytes 8 | tf_op jit(solution)/shard_map/psum | solution.py:213
  565.9 13.6 %all-gather.6 = f32[32,2,1024]{2,1,0:T(2,128)S(1)} all-gather(f32[4,2,1024]{2,1,0:T(2,128)S(1)} %copy.309), channel_id=8, replica_groups=mesh['brick'=8,'grp'=16] {'brick'}, dimensions={0}, use_global_device_ids=true | all-gather | bytes 294912 | tf_op jit(solution)/shard_map/all_gather | solution.py:122
  588.0 7.3 multiply_add_fusion.1
  603.4 2.7 pad_maximum_fusion.6
  607.5 2.5 broadcast_in_dim.764
  620.1 2.5 concatenate.791
  630.3 2.5 broadcast_in_dim.760
  637.4 3.3 multiply_reduce_fusion.1
  640.7 66.1 %psum.45 = f32[]{:T(128)} all-reduce(f32[]{:T(128)} %get-tuple-element.50), channel_id=1, replica_groups=mesh['brick'=8,'grp'=16] {'brick','grp'}, use_global_device_ids=true, to_apply=%region_26.29 | all-reduce | flops 1 | bytes 8 | tf_op jit(solution)/shard_map/psum | solution.py:213
  711.4 13.5 %all-gather.7 = f32[32,2,1024]{2,1,0:T(2,128)S(1)} all-gather(f32[4,2,1024]{2,1,0:T(2,128)S(1)} %copy.314), channel_id=9, replica_groups=mesh['brick'=8,'grp'=16] {'brick'}, dimensions={0}, use_global_device_ids=true | all-gather | bytes 294912 | tf_op jit(solution)/shard_map/all_gather | solution.py:122
  733.8 8.2 multiply_divide_fusion
  747.8 31.5 %all-reduce.20 = f32[32]{0:T(128)} all-reduce(f32[32]{0:T(128)} %dynamic-update-slice.5), channel_id=10, replica_groups=mesh['brick'=8,'grp'=16] {'grp'}, use_global_device_ids=true, to_apply=%add.20 | all-reduce | flops 32 | bytes 256 | tf_op jit(solution)/shard_map/triangular_solve/reshape.87 | solution.py:197
  788.1 3.0 pad_maximum_fusion.8
  823.6 2.4 broadcast_in_dim.771
  831.9 3.8 multiply_reduce_fusion
  835.8 70.9 %psum.46 = f32[]{:T(128)} all-reduce(f32[]{:T(128)} %get-tuple-element.42), channel_id=1, replica_groups=mesh['brick'=8,'grp'=16] {'brick','grp'}, use_global_device_ids=true, to_apply=%region_30.33 | all-reduce | flops 1 | bytes 8 | tf_op jit(solution)/shard_map/psum | solution.py:213
  914.6 13.8 %all-gather.9 = f32[32,2,1024]{2,1,0:T(2,128)S(1)} all-gather(f32[4,2,1024]{2,1,0:T(2,128)S(1)} %copy.319), channel_id=11, replica_groups=mesh['brick'=8,'grp'=16] {'brick'}, dimensions={0}, use_global_device_ids=true | all-gather | bytes 294912 | tf_op jit(solution)/shard_map/all_gather | solution.py:122
  938.2 10.7 %multiply_add_fusion = f32[2,32,32,32]{3,2,1,0:T(8,128)S(1)} fusion(f32[2,32,32,32]{3,2,1,0:T(8,128)} %copy-done.5, f32[2,32,32,32]{3,2,1,0:T(8,128)} %get-tuple-element.75, f32[2,32,32,32]{3,2,1,0:T(8,128)} %get-tuple-element.77, f32[2,32,32,32]{3,2,1,0:T(8,128)} %get-tuple-element.76, f32[2,32,32,32]{3,2,1,0:T(8,128)} %concatenate.773, ...), kind=kLoop, calls=%fused_computation.76 | loop fusion | flops 3735552 | bytes 5865592 | tf_op jit(solution)/shard_map/add | solution.py:225
  959.3 2.4 broadcast_in_dim.783
  966.9 2.4 concatenate.818
  969.3 2.4 concatenate.775
  978.0 2.5 broadcast_in_dim.779
  984.3 2.6 fusion.155
  988.6 66.6 %psum.47 = f32[]{:T(128)} all-reduce(f32[]{:T(128)} %fusion.155), channel_id=1, replica_groups=mesh['brick'=8,'grp'=16] {'brick','grp'}, use_global_device_ids=true, to_apply=%region_33.36 | all-reduce | flops 1 | bytes 8 | tf_op jit(solution)/shard_map/psum | solution.py:213
  1056.6 6.0 fusion.149
  (713 shorter events, 371.7 us)
Async XLA Ops:
  0.6 9.8 copy-start.37
  0.6 11.2 %copy-start = (f32[1,1,6,2,32,1024]{5,4,3,2,1,0:T(8,128)S(1)}, f32[1,1,6,2,32,1024]{5,4,3,2,1,0:T(8,128)}, u32[]{:S(2)}) copy-start(f32[1,1,6,2,32,1024]{5,4,3,2,1,0:T(8,128)} %param.11) | copy-start | bytes 4718596
  4.7 34.9 %copy-start.95 = (pred[32]{0:T(512)(128)(4,1)}, pred[32]{0:T(512)(128)(4,1)S(1)}, u32[]{:S(2)}) copy-start(pred[32]{0:T(512)(128)(4,1)S(1)} %get-tuple-element.277) | copy-start | bytes 100
  4.7 34.9 %copy-start.101 = (pred[32]{0:T(512)(128)(4,1)}, pred[32]{0:T(512)(128)(4,1)S(1)}, u32[]{:S(2)}) copy-start(pred[32]{0:T(512)(128)(4,1)S(1)} %get-tuple-element.278) | copy-start | bytes 100
  8.2 31.4 %copy-start.85 = (f32[2]{0:T(128)}, f32[2]{0:T(128)S(1)}, u32[]{:S(2)}) copy-start(f32[2]{0:T(128)S(1)} %get-tuple-element.32) | copy-start | bytes 28
  22.2 17.4 %copy-start.118 = (f32[2]{0:T(128)}, f32[2]{0:T(128)S(1)}, u32[]{:S(2)}) copy-start(f32[2]{0:T(128)S(1)} %get-tuple-element.268) | copy-start | bytes 28
  27.9 10.7 %copy-start.20 = (f32[1,1,2,32,1024]{4,3,2,1,0:T(8,128)S(1)}, f32[1,1,2,32,1024]{4,3,2,1,0:T(8,128)}, u32[]{:S(2)}) copy-start(f32[1,1,2,32,1024]{4,3,2,1,0:T(8,128)} %param.9) | copy-start | bytes 786436
  28.0 11.6 %copy-start.38 = (f32[1,1,2,32,1024]{4,3,2,1,0:T(8,128)S(1)}, f32[1,1,2,32,1024]{4,3,2,1,0:T(8,128)}, u32[]{:S(2)}) copy-start(f32[1,1,2,32,1024]{4,3,2,1,0:T(8,128)} %param.10) | copy-start | bytes 786436
  28.0 11.6 %copy-start.122 = (f32[2]{0:T(128)S(1)}, f32[2]{0:T(128)}, u32[]{:S(2)}) copy-start(f32[2]{0:T(128)} %copy-done.121) | copy-start | bytes 28
  28.0 11.6 %copy-start.125 = (f32[2]{0:T(128)S(1)}, f32[2]{0:T(128)}, u32[]{:S(2)}) copy-start(f32[2]{0:T(128)} %copy-done.124) | copy-start | bytes 28
  28.0 11.6 %copy-start.130 = (f32[2]{0:T(128)S(1)}, f32[2]{0:T(128)}, u32[]{:S(2)}) copy-start(f32[2]{0:T(128)} %copy-done.129) | copy-start | bytes 28
  28.0 11.6 %copy-start.134 = (f32[2]{0:T(128)S(1)}, f32[2]{0:T(128)}, u32[]{:S(2)}) copy-start(f32[2]{0:T(128)} %copy-done.133) | copy-start | bytes 28
  28.0 11.6 %copy-start.138 = (f32[2]{0:T(128)S(1)}, f32[2]{0:T(128)}, u32[]{:S(2)}) copy-start(f32[2]{0:T(128)} %copy-done.137) | copy-start | bytes 28
  30.5 121.8 %collective-permute-start.1 = (f32[1,2,1024]{2,1,0:T(2,128)}, f32[1,2,1024]{2,1,0:T(2,128)}, u32[]{:S(2)}, u32[]{:S(2)}) collective-permute-start(f32[1,2,1024]{2,1,0:T(2,128)} %stack_reshape_squeeze.37), channel_id=1, source_target_pairs={{0,1},{1,2},{2,3},{3,4},{4,5},{5,6},{6,7},{7,8},{8,9},{9,10},{10,1... | collective-permute-start | bytes 24584 | tf_op jit(solution)/shard_map/ppermute | solution.py:18
  36.1 115.4 %collective-permute-start = (f32[1,2,1024]{2,1,0:T(2,128)}, f32[1,2,1024]{2,1,0:T(2,128)}, u32[]{:S(2)}, u32[]{:S(2)}) collective-permute-start(f32[1,2,1024]{2,1,0:T(2,128)} %stack_reshape_squeeze.36), channel_id=1, source_target_pairs={{1,0},{2,1},{3,2},{4,3},{5,4},{6,5},{7,6},{8,7},{9,8},{10,9},{11,1... | collective-permute-start | bytes 24584 | tf_op jit(solution)/shard_map/ppermute | solution.py:21
  40.7 19.9 %copy-start.31 = (f32[2,32,1024]{2,1,0:T(8,128)}, f32[2,32,1024]{2,1,0:T(8,128)S(1)}, u32[]{:S(2)}) copy-start(f32[2,32,1024]{2,1,0:T(8,128)S(1)} %get-tuple-element.68) | copy-start | bytes 786436
  40.7 27.0 %copy-start.13 = (f32[2,32,1024]{2,1,0:T(8,128)}, f32[2,32,1024]{2,1,0:T(8,128)S(1)}, u32[]{:S(2)}) copy-start(f32[2,32,1024]{2,1,0:T(8,128)S(1)} %get-tuple-element.73) | copy-start | bytes 786436
  40.7 446.4 %copy-start.11 = (f32[2,32,1024]{2,1,0:T(8,128)}, f32[2,32,1024]{2,1,0:T(8,128)S(1)}, u32[]{:S(2)}) copy-start(f32[2,32,1024]{2,1,0:T(8,128)S(1)} %get-tuple-element.72) | copy-start | bytes 786436
  44.2 16.4 %copy-start.141 = (pred[8,4]{1,0:T(8,128)(4,1)}, pred[8,4]{1,0:T(8,128)(4,1)S(1)}, u32[]{:S(2)}) copy-start(pred[8,4]{1,0:T(8,128)(4,1)S(1)} %iota_compare_fusion.11) | copy-start | bytes 100
  68.2 21.3 %copy-start.7 = (f32[2,32,32,32]{3,2,1,0:T(8,128)S(1)}, f32[2,32,32,32]{3,2,1,0:T(8,128)}, u32[]{:S(2)}) copy-start(f32[2,32,32,32]{3,2,1,0:T(8,128)} %copy-done.6) | copy-start | bytes 786436
  89.5 47.8 %copy-start.59 = (f32[2,32,992]{2,1,0:T(8,128)S(1)}, f32[2,32,992]{2,1,0:T(8,128)}, u32[]{:S(2)}) copy-start(f32[2,32,992]{2,1,0:T(8,128)} %get-tuple-element.146) | copy-start | bytes 761860
  91.3 53.5 %copy-start.96 = (pred[32]{0:T(512)(128)(4,1)S(1)}, pred[32]{0:T(512)(128)(4,1)}, u32[]{:S(2)}) copy-start(pred[32]{0:T(512)(128)(4,1)} %copy-done.95) | copy-start | bytes 100
  91.3 54.2 %copy-start.102 = (pred[32]{0:T(512)(128)(4,1)S(1)}, pred[32]{0:T(512)(128)(4,1)}, u32[]{:S(2)}) copy-start(pred[32]{0:T(512)(128)(4,1)} %copy-done.101) | copy-start | bytes 100
  126.0 22.8 %copy-start.81 = (f32[2,32,32]{2,1,0:T(8,128)}, f32[2,32,32]{2,1,0:T(8,128)S(1)}, u32[]{:S(2)}) copy-start(f32[2,32,32]{2,1,0:T(8,128)S(1)} %reshape.2206) | copy-start | bytes 24580
  126.8 22.1 %copy-start.82 = (f32[2,32,32]{2,1,0:T(8,128)}, f32[2,32,32]{2,1,0:T(8,128)S(1)}, u32[]{:S(2)}) copy-start(f32[2,32,32]{2,1,0:T(8,128)S(1)} %reshape.2205) | copy-start | bytes 24580
  137.4 11.5 %copy-start.57 = (f32[2,31,1024]{2,1,0:T(8,128)S(1)}, f32[2,31,1024]{2,1,0:T(8,128)}, u32[]{:S(2)}) copy-start(f32[2,31,1024]{2,1,0:T(8,128)} %get-tuple-element.142) | copy-start | bytes 761860
  138.6 14.4 %copy-start.156 = (f32[2]{0:T(128)}, f32[2]{0:T(128)S(1)}, u32[]{:S(2)}) copy-start(f32[2]{0:T(128)S(1)} %fusion.180) | copy-start | bytes 28
  221.3 44.6 %collective-permute-start.3 = (f32[1,2,1024]{2,1,0:T(2,128)}, f32[1,2,1024]{2,1,0:T(2,128)}, u32[]{:S(2)}, u32[]{:S(2)}) collective-permute-start(f32[1,2,1024]{2,1,0:T(2,128)} %stack_reshape_squeeze.39), channel_id=1, source_target_pairs={{0,1},{1,2},{2,3},{3,4},{4,5},{5,6},{6,7},{7,8},{8,9},{9,10},{10,1... | collective-permute-start | bytes 24584 | tf_op jit(solution)/shard_map/ppermute | solution.py:18
  223.2 51.0 %collective-permute-start.2 = (f32[1,2,1024]{2,1,0:T(2,128)}, f32[1,2,1024]{2,1,0:T(2,128)}, u32[]{:S(2)}, u32[]{:S(2)}) collective-permute-start(f32[1,2,1024]{2,1,0:T(2,128)} %stack_reshape_squeeze.38), channel_id=1, source_target_pairs={{1,0},{2,1},{3,2},{4,3},{5,4},{6,5},{7,6},{8,7},{9,8},{10,9},{11,1... | collective-permute-start | bytes 24584 | tf_op jit(solution)/shard_map/ppermute | solution.py:21
  359.8 19.8 %copy-start.34 = (f32[2,32,1024]{2,1,0:T(8,128)S(1)}, f32[2,32,1024]{2,1,0:T(8,128)}, u32[]{:S(2)}) copy-start(f32[2,32,1024]{2,1,0:T(8,128)} %copy-done.33) | copy-start | bytes 786436
  436.2 39.2 %collective-permute-start.5 = (f32[1,2,1024]{2,1,0:T(2,128)}, f32[1,2,1024]{2,1,0:T(2,128)}, u32[]{:S(2)}, u32[]{:S(2)}) collective-permute-start(f32[1,2,1024]{2,1,0:T(2,128)} %stack_reshape_squeeze.41), channel_id=1, source_target_pairs={{0,1},{1,2},{2,3},{3,4},{4,5},{5,6},{6,7},{7,8},{8,9},{9,10},{10,1... | collective-permute-start | bytes 24584 | tf_op jit(solution)/shard_map/ppermute | solution.py:18
  438.1 43.2 %collective-permute-start.4 = (f32[1,2,1024]{2,1,0:T(2,128)}, f32[1,2,1024]{2,1,0:T(2,128)}, u32[]{:S(2)}, u32[]{:S(2)}) collective-permute-start(f32[1,2,1024]{2,1,0:T(2,128)} %stack_reshape_squeeze.40), channel_id=1, source_target_pairs={{1,0},{2,1},{3,2},{4,3},{5,4},{6,5},{7,6},{8,7},{9,8},{10,9},{11,1... | collective-permute-start | bytes 24584 | tf_op jit(solution)/shard_map/ppermute | solution.py:21
  599.9 27.8 %collective-permute-start.7 = (f32[1,2,1024]{2,1,0:T(2,128)}, f32[1,2,1024]{2,1,0:T(2,128)}, u32[]{:S(2)}, u32[]{:S(2)}) collective-permute-start(f32[1,2,1024]{2,1,0:T(2,128)} %stack_reshape_squeeze.43), channel_id=1, source_target_pairs={{0,1},{1,2},{2,3},{3,4},{4,5},{5,6},{6,7},{7,8},{8,9},{9,10},{10,1... | collective-permute-start | bytes 24584 | tf_op jit(solution)/shard_map/ppermute | solution.py:18
  602.1 30.7 %collective-permute-start.6 = (f32[1,2,1024]{2,1,0:T(2,128)}, f32[1,2,1024]{2,1,0:T(2,128)}, u32[]{:S(2)}, u32[]{:S(2)}) collective-permute-start(f32[1,2,1024]{2,1,0:T(2,128)} %stack_reshape_squeeze.42), channel_id=1, source_target_pairs={{1,0},{2,1},{3,2},{4,3},{5,4},{6,5},{7,6},{8,7},{9,8},{10,9},{11,1... | collective-permute-start | bytes 24584 | tf_op jit(solution)/shard_map/ppermute | solution.py:21
  607.5 10.3 copy-start.22
  637.4 70.8 %copy-start.45 = (f32[2,32,1024]{2,1,0:T(8,128)S(1)}, f32[2,32,1024]{2,1,0:T(8,128)}, u32[]{:S(2)}) copy-start(f32[2,32,1024]{2,1,0:T(8,128)} %copy-done.44) | copy-start | bytes 786436
  709.7 18.3 %copy-start.54 = (f32[2,32,1024]{2,1,0:T(8,128)}, f32[2,32,1024]{2,1,0:T(8,128)S(1)}, u32[]{:S(2)}) copy-start(f32[2,32,1024]{2,1,0:T(8,128)S(1)} %get-tuple-element.47) | copy-start | bytes 786436
  783.5 36.6 %collective-permute-start.9 = (f32[1,2,1024]{2,1,0:T(2,128)}, f32[1,2,1024]{2,1,0:T(2,128)}, u32[]{:S(2)}, u32[]{:S(2)}) collective-permute-start(f32[1,2,1024]{2,1,0:T(2,128)} %stack_reshape_squeeze.45), channel_id=1, source_target_pairs={{0,1},{1,2},{2,3},{3,4},{4,5},{5,6},{6,7},{7,8},{8,9},{9,10},{10,1... | collective-permute-start | bytes 24584 | tf_op jit(solution)/shard_map/ppermute | solution.py:18
  785.4 40.6 %collective-permute-start.8 = (f32[1,2,1024]{2,1,0:T(2,128)}, f32[1,2,1024]{2,1,0:T(2,128)}, u32[]{:S(2)}, u32[]{:S(2)}) collective-permute-start(f32[1,2,1024]{2,1,0:T(2,128)} %stack_reshape_squeeze.44), channel_id=1, source_target_pairs={{1,0},{2,1},{3,2},{4,3},{5,4},{6,5},{7,6},{8,7},{9,8},{10,9},{11,1... | collective-permute-start | bytes 24584 | tf_op jit(solution)/shard_map/ppermute | solution.py:21
  823.6 8.3 copy-start.108
  823.6 8.3 copy-start.110
  823.6 8.3 copy-start.120
  913.2 19.4 %copy-start.36 = (f32[2,32,1024]{2,1,0:T(8,128)S(1)}, f32[2,32,1024]{2,1,0:T(8,128)}, u32[]{:S(2)}) copy-start(f32[2,32,1024]{2,1,0:T(8,128)} %copy-done.35) | copy-start | bytes 786436
  952.7 22.7 %collective-permute-start.11 = (f32[1,2,1024]{2,1,0:T(2,128)S(1)}, f32[1,2,1024]{2,1,0:T(2,128)S(1)}, u32[]{:S(2)}, u32[]{:S(2)}) collective-permute-start(f32[1,2,1024]{2,1,0:T(2,128)S(1)} %stack_reshape_squeeze.47), channel_id=1, source_target_pairs={{0,1},{1,2},{2,3},{3,4},{4,5},{5,6},{6,7},{7,8},{8,9},{9,10},{10,1... | collective-permute-start | bytes 24584 | tf_op jit(solution)/shard_map/ppermute | solution.py:18
  954.2 26.3 %collective-permute-start.10 = (f32[1,2,1024]{2,1,0:T(2,128)S(1)}, f32[1,2,1024]{2,1,0:T(2,128)S(1)}, u32[]{:S(2)}, u32[]{:S(2)}) collective-permute-start(f32[1,2,1024]{2,1,0:T(2,128)S(1)} %stack_reshape_squeeze.46), channel_id=1, source_target_pairs={{1,0},{2,1},{3,2},{4,3},{5,4},{6,5},{7,6},{8,7},{9,8},{10,9},{11,1... | collective-permute-start | bytes 24584 | tf_op jit(solution)/shard_map/ppermute | solution.py:21
  984.3 72.3 %copy-start.40 = (f32[1,1,2,32,1024]{4,3,2,1,0:T(8,128)S(1)}, f32[1,1,2,32,1024]{4,3,2,1,0:T(8,128)}, u32[]{:S(2)}) copy-start(f32[1,1,2,32,1024]{4,3,2,1,0:T(8,128)} %param.10) | copy-start | bytes 786436
  984.3 72.3 %copy-start.75 = (pred[32,1024]{1,0:T(8,128)(4,1)S(1)}, pred[32,1024]{1,0:T(8,128)(4,1)}, u32[]{:S(2)}) copy-start(pred[32,1024]{1,0:T(8,128)(4,1)} %copy-done.73) | copy-start | bytes 98308
  984.3 72.3 %copy-start.78 = (pred[32,1024]{1,0:T(8,128)(4,1)S(1)}, pred[32,1024]{1,0:T(8,128)(4,1)}, u32[]{:S(2)}) copy-start(pred[32,1024]{1,0:T(8,128)(4,1)} %copy-done.76) | copy-start | bytes 98308
  (131 other events, 441.1 us)
where the time goes:
time: 1080 us; the launch traced here: 1060 us
  blocking collectives  547 us (51%)
  local copies, waits for them, and re-layouts  336 us (31%)
  other arithmetic  139 us (13%)
  starting transfers between devices  22.6 us (2%)
  between operations  15.9 us (1%)
    psum x5, blocking collectives, global_sum(): return lax.psum(jnp.sum(values), ('brick', 'grp'))  339 us
    another operation x3, blocking collectives, coarse_solve(): lax.linalg.triangular_solve(factor, gathered_terms, left_side=True, lower...  94.1 us
    all_gather x6, blocking collectives, apply_operator(): portion = lax.all_gather(outgoing_sides[None], 'brick', axis=0, tiled=True)  94.1 us
    broadcast_in_dim x26, local copies, waits for them, and re-layouts, apply_operator(): jnp.where(cube_third == BS - 1, from_above, jnp.roll(cube, -1, axis=3))  45 us
    broadcast_in_dim x26, local copies, waits for them, and re-layouts, apply_operator(): jnp.where(cube_third == 0, from_below, jnp.roll(cube, 1, axis=3))  43.7 us
    concatenate x12, local copies, waits for them, and re-layouts, apply_operator(): jnp.roll(cube, -1, axis=3)  26.6 us
    concatenate x12, local copies, waits for them, and re-layouts, apply_operator(): jnp.roll(cube, 1, axis=3)  25.4 us
    div x6, other arithmetic, precondition(): smoothed = OMEGA * residual_field / diagonal  24.1 us
  transfers between devices with their start and end apart: 12, of which 0 were waited for; matrix products, arithmetic and copies ran while one was open for 21% of the time, Pallas kernels for 0%

commit v1 on v0

--- a/solution.py
+++ b/solution.py
@@ -2,6 +2,7 @@
 import jax.numpy as jnp
 from jax import lax
 from jax.sharding import PartitionSpec as P
+from jax.lax import all_to_all, psum
 
 BS = 32
 PATCH_X = 1
@@ -119,7 +120,16 @@
                 pad_rows(grid_upper_y[:, PATCH_Y - 1], capacity),
             ]
         )
-        portion = lax.all_gather(outgoing_sides[None], "brick", axis=0, tiled=True)
+        original = outgoing_sides[None]
+        portion = jnp.concatenate(
+            all_to_all(
+                jnp.stack([original for _ in range(psum(1, axis_name="brick"))], axis=0),
+                axis_name="brick",
+                split_axis=0,
+                concat_axis=0,
+            ),
+            axis=0,
+        )
         sources = jnp.arange(portion.shape[0], dtype=jnp.int32)
         matches = sources[:, None] == wanted[None, :]
         remote = jnp.zeros((4, capacity, face_size), jnp.float32) + jnp.sum(

time: 1080 us -> 1050 us (0.972)
  blocking collectives: 547 us -> 441 us
  starting transfers between devices: 22.6 us -> 84.3 us
  other arithmetic: 139 us -> 150 us
    all_gather x6 -> x0, blocking collectives: 94.1 us -> none  [apply_operator(): portion = lax.all_gather(outgoing_sides[None], 'brick', axis=0, tiled=True)]
    all_to_all x0 -> x6, starting transfers between devices: none -> 56.6 us  [apply_operator(): all_to_all(jnp.stack([original for _ in range(psum(1, axis_name='brick'))...]
    psum x5, blocking collectives: 339 us -> 327 us  [global_sum(): return lax.psum(jnp.sum(values), ('brick', 'grp'))]
    another operation x3 -> x22, local copies, waits for them, and re-layouts: 1.1 us -> 12.7 us  [the longest x6 4.73 us: apply_operator(): jnp.stack([original for _ in range(psum(1, axis_name='brick'))], axis=0)]
    unnamed x350 -> x328, local copies, waits for them, and re-layouts: 19.7 us -> 8.4 us
    concatenate x14 -> x24, local copies, waits for them, and re-layouts: 20.9 us -> 29.6 us  [apply_operator(): jnp.concatenate([field[:, 1:, :], beyond_xplus[:, None, :]], axis=1)]
  transfers between devices with their start and end apart: 12 -> 18, of which waited for: 0 -> 0; matrix products, arithmetic and copies ran while one was open for 21% -> 25% of each run, Pallas kernels for 0% -> 0%
where the time goes in v1:
time: 1050 us; the launch traced here: 1030 us
  blocking collectives  441 us (42%)
  local copies, waits for them, and re-layouts  339 us (32%)
  other arithmetic  150 us (14%)
  starting transfers between devices  84.3 us (8%)
  between operations  15 us (1%)
    psum x5, blocking collectives, global_sum(): return lax.psum(jnp.sum(values), ('brick', 'grp'))  327 us
    another operation x3, blocking collectives, coarse_solve(): lax.linalg.triangular_solve(factor, gathered_terms, left_side=True, lower...  94.1 us
    all_to_all x6, starting transfers between devices, apply_operator(): all_to_all(jnp.stack([original for _ in range(psum(1, axis_name='brick'))...  56.6 us
    broadcast_in_dim x26, local copies, waits for them, and re-layouts, apply_operator(): jnp.where(cube_third == BS - 1, from_above, jnp.roll(cube, -1, axis=3))  43 us
    broadcast_in_dim x26, local copies, waits for them, and re-layouts, apply_operator(): jnp.where(cube_third == 0, from_below, jnp.roll(cube, 1, axis=3))  36 us
    concatenate x24, local copies, waits for them, and re-layouts, apply_operator(): jnp.concatenate([field[:, 1:, :], beyond_xplus[:, None, :]], axis=1)  29.6 us
    concatenate x12, local copies, waits for them, and re-layouts, apply_operator(): jnp.roll(cube, -1, axis=3)  26.6 us
    div x6, other arithmetic, precondition(): smoothed = OMEGA * residual_field / diagonal  25.5 us
  transfers between devices with their start and end apart: 18, of which 0 were waited for; matrix products, arithmetic and copies ran while one was open for 25% of the time, Pallas kernels for 0%

profile of v1, /device:TPU:1, one launch (start us, length us, event | category | flops | bytes accessed | tf_op | source)
XLA Modules:
  0.0 1031.8 jit_solution(8979715707319562568)
XLA Ops:
  6.4 2.6 multiply_divide_fusion.5
  11.5 6.1 all-to-all-start
  27.6 2.4 squeeze.120
  38.6 5.7 multiply_divide_fusion.2
  46.8 4.1 collective-permute-start.1
  63.4 19.9 %all-gather.4 = f32[16,4,2]{1,2,0:T(2,128)S(1)} all-gather(f32[1,4,2]{1,2,0:T(2,128)S(1)} %bitcast.582), channel_id=2, replica_groups=mesh['brick'=8,'grp'=16] {'grp'}, dimensions={0}, use_global_device_ids=true | all-gather | bytes 544 | tf_op jit(solution)/shard_map/all_gather | solution.py:199
  88.8 31.0 %all-reduce.18 = f32[32]{0:T(128)S(1)} all-reduce(f32[32]{0:T(128)S(1)} %dynamic-update-slice.3), channel_id=3, replica_groups=mesh['brick'=8,'grp'=16] {'grp'}, use_global_device_ids=true, to_apply=%add.18 | all-reduce | flops 32 | bytes 256 | tf_op jit(solution)/shard_map/triangular_solve/reshape.99 | solution.py:207
  123.3 2.9 cholesky.19
  127.5 2.4 custom-call.14
  158.8 8.4 fusion.46
  167.2 2.4 concatenate.643
  189.7 17.8 %all-to-all-start.1 = ((f32[8,1,4,2,1024]{4,3,2,1,0:T(2,128)}), f32[8,1,4,2,1024]{4,3,2,1,0:T(2,128)}, u32[]{:S(2)}, u32[]{:S(2)}) async-start(f32[8,1,4,2,1024]{4,3,2,1,0:T(2,128)} %stack.147), calls=%async_computation.1 | async-start | bytes 524288 | tf_op jit(solution)/shard_map/all_to_all | solution.py:125
  213.7 3.0 pad_maximum_fusion.2
  220.9 2.4 concatenate.676
  233.0 2.4 concatenate.663
  271.1 3.9 multiply_reduce_fusion.3
  274.9 64.7 %all-reduce.21 = (f32[]{:T(128)}, f32[]{:T(128)}) all-reduce(f32[]{:T(128)} %get-tuple-element.17, f32[]{:T(128)} %get-tuple-element.16), channel_id=1, replica_groups=mesh['brick'=8,'grp'=16] {'brick','grp'}, use_global_device_ids=true, to_apply=%region_16.19 | all-reduce | flops 2 | bytes 16 | tf_op jit(solution)/shard_map/psum | solution.py:223
  353.6 8.9 multiply_divide_fusion.1
  369.6 31.3 %all-reduce.19 = f32[32]{0:T(128)} all-reduce(f32[32]{0:T(128)} %dynamic-update-slice.4), channel_id=4, replica_groups=mesh['brick'=8,'grp'=16] {'grp'}, use_global_device_ids=true, to_apply=%add.19 | all-reduce | flops 32 | bytes 256 | tf_op jit(solution)/shard_map/triangular_solve/reshape.99 | solution.py:207
  410.2 11.8 %all-to-all-start.2 = ((f32[8,1,4,2,1024]{4,3,2,1,0:T(2,128)}), f32[8,1,4,2,1024]{4,3,2,1,0:T(2,128)}, u32[]{:S(2)}, u32[]{:S(2)}) async-start(f32[8,1,4,2,1024]{4,3,2,1,0:T(2,128)} %stack.153), calls=%async_computation.2 | async-start | bytes 524288 | tf_op jit(solution)/shard_map/all_to_all | solution.py:125
  428.9 3.1 pad_maximum_fusion.4
  432.2 3.4 fusion.96
  444.8 2.4 concatenate.695
  477.4 3.8 multiply_reduce_fusion.2
  481.1 64.5 %psum.44 = f32[]{:T(128)} all-reduce(f32[]{:T(128)} %get-tuple-element.50), channel_id=1, replica_groups=mesh['brick'=8,'grp'=16] {'brick','grp'}, use_global_device_ids=true, to_apply=%region_23.26 | all-reduce | flops 1 | bytes 8 | tf_op jit(solution)/shard_map/psum | solution.py:223
  558.4 7.2 multiply_add_fusion.1
  571.3 4.6 all-to-all-start.3
  577.2 4.8 collective-permute-start.7
  583.5 2.7 pad_maximum_fusion.6
  591.4 2.5 concatenate.791
  607.5 2.5 broadcast_in_dim.756
  616.9 3.4 multiply_reduce_fusion.1
  620.3 66.2 %psum.45 = f32[]{:T(128)} all-reduce(f32[]{:T(128)} %get-tuple-element.46), channel_id=1, replica_groups=mesh['brick'=8,'grp'=16] {'brick','grp'}, use_global_device_ids=true, to_apply=%region_26.29 | all-reduce | flops 1 | bytes 8 | tf_op jit(solution)/shard_map/psum | solution.py:223
  701.1 8.2 multiply_divide_fusion
  715.1 31.7 %all-reduce.20 = f32[32]{0:T(128)} all-reduce(f32[32]{0:T(128)} %dynamic-update-slice.5), channel_id=5, replica_groups=mesh['brick'=8,'grp'=16] {'grp'}, use_global_device_ids=true, to_apply=%add.20 | all-reduce | flops 32 | bytes 256 | tf_op jit(solution)/shard_map/triangular_solve/reshape.99 | solution.py:207
  752.7 11.8 %all-to-all-start.4 = ((f32[8,1,4,2,1024]{4,3,2,1,0:T(2,128)}), f32[8,1,4,2,1024]{4,3,2,1,0:T(2,128)}, u32[]{:S(2)}, u32[]{:S(2)}) async-start(f32[8,1,4,2,1024]{4,3,2,1,0:T(2,128)} %stack.165), calls=%async_computation.4 | async-start | bytes 524288 | tf_op jit(solution)/shard_map/all_to_all | solution.py:125
  770.5 3.0 pad_maximum_fusion.8
  781.7 2.4 concatenate.805
  806.6 2.4 broadcast_in_dim.745
  818.0 3.8 multiply_reduce_fusion
  821.7 64.4 %psum.46 = f32[]{:T(128)} all-reduce(f32[]{:T(128)} %get-tuple-element.38), channel_id=1, replica_groups=mesh['brick'=8,'grp'=16] {'brick','grp'}, use_global_device_ids=true, to_apply=%region_30.33 | all-reduce | flops 1 | bytes 8 | tf_op jit(solution)/shard_map/psum | solution.py:223
  899.1 10.7 %multiply_add_fusion = f32[2,32,32,32]{3,2,1,0:T(8,128)S(1)} fusion(f32[2,32,32,32]{3,2,1,0:T(8,128)} %copy-done.5, f32[2,32,32,32]{3,2,1,0:T(8,128)} %get-tuple-element.71, f32[2,32,32,32]{3,2,1,0:T(8,128)} %get-tuple-element.73, f32[2,32,32,32]{3,2,1,0:T(8,128)} %get-tuple-element.72, f32[2,32,32,32]{3,2,1,0:T(8,128)} %concatenate.773, ...), kind=kLoop, calls=%fused_computation.76 | loop fusion | flops 3735552 | bytes 5865592 | tf_op jit(solution)/shard_map/add | solution.py:235
  915.8 4.6 all-to-all-start.5
  920.5 4.4 collective-permute-start.11
  944.0 2.5 broadcast_in_dim.760
  954.1 2.6 fusion.161
  956.8 66.7 %psum.47 = f32[]{:T(128)} all-reduce(f32[]{:T(128)} %fusion.161), channel_id=1, replica_groups=mesh['brick'=8,'grp'=16] {'brick','grp'}, use_global_device_ids=true, to_apply=%region_33.36 | all-reduce | flops 1 | bytes 8 | tf_op jit(solution)/shard_map/psum | solution.py:223
  1024.8 6.0 fusion.149
  (730 shorter events, 386.0 us)
Async XLA Ops:
  4.5 34.1 %copy-start.93 = (pred[32]{0:T(512)(128)(4,1)}, pred[32]{0:T(512)(128)(4,1)S(1)}, u32[]{:S(2)}) copy-start(pred[32]{0:T(512)(128)(4,1)S(1)} %iota_compare_fusion.13) | copy-start | bytes 100
  4.5 34.1 %copy-start.98 = (pred[32]{0:T(512)(128)(4,1)}, pred[32]{0:T(512)(128)(4,1)S(1)}, u32[]{:S(2)}) copy-start(pred[32]{0:T(512)(128)(4,1)S(1)} %iota_compare_fusion.12) | copy-start | bytes 100
  5.7 48.4 %copy-start.79 = (f32[2]{0:T(128)}, f32[2]{0:T(128)S(1)}, u32[]{:S(2)}) copy-start(f32[2]{0:T(128)S(1)} %get-tuple-element.28) | copy-start | bytes 28
  5.9 32.7 %copy-start.117 = (f32[2]{0:T(128)}, f32[2]{0:T(128)S(1)}, u32[]{:S(2)}) copy-start(f32[2]{0:T(128)S(1)} %get-tuple-element.262) | copy-start | bytes 28
  6.4 14.8 %copy-start.20 = (f32[1,1,2,32,1024]{4,3,2,1,0:T(8,128)S(1)}, f32[1,1,2,32,1024]{4,3,2,1,0:T(8,128)}, u32[]{:S(2)}) copy-start(f32[1,1,2,32,1024]{4,3,2,1,0:T(8,128)} %param.9) | copy-start | bytes 786436
  9.1 14.8 %copy-start.31 = (f32[2,32,1024]{2,1,0:T(8,128)}, f32[2,32,1024]{2,1,0:T(8,128)S(1)}, u32[]{:S(2)}) copy-start(f32[2,32,1024]{2,1,0:T(8,128)S(1)} %get-tuple-element.64) | copy-start | bytes 786436
  9.1 53.4 %copy-start.13 = (f32[2,32,1024]{2,1,0:T(8,128)}, f32[2,32,1024]{2,1,0:T(8,128)S(1)}, u32[]{:S(2)}) copy-start(f32[2,32,1024]{2,1,0:T(8,128)S(1)} %get-tuple-element.69) | copy-start | bytes 786436
  9.1 468.3 %copy-start.11 = (f32[2,32,1024]{2,1,0:T(8,128)}, f32[2,32,1024]{2,1,0:T(8,128)S(1)}, u32[]{:S(2)}) copy-start(f32[2,32,1024]{2,1,0:T(8,128)S(1)} %get-tuple-element.68) | copy-start | bytes 786436
  9.1 13.5 %copy-start.32 = (f32[1,1,2,32,1024]{4,3,2,1,0:T(8,128)S(1)}, f32[1,1,2,32,1024]{4,3,2,1,0:T(8,128)}, u32[]{:S(2)}) copy-start(f32[1,1,2,32,1024]{4,3,2,1,0:T(8,128)} %param.10) | copy-start | bytes 786436
  11.5 12.4 %copy-start = (f32[1,1,6,2,32,1024]{5,4,3,2,1,0:T(8,128)S(1)}, f32[1,1,6,2,32,1024]{5,4,3,2,1,0:T(8,128)}, u32[]{:S(2)}) copy-start(f32[1,1,6,2,32,1024]{5,4,3,2,1,0:T(8,128)} %param.11) | copy-start | bytes 4718596
  11.5 136.8 %all-to-all-start = ((f32[8,1,4,2,1024]{4,3,2,1,0:T(2,128)}), f32[8,1,4,2,1024]{4,3,2,1,0:T(2,128)}, u32[]{:S(2)}, u32[]{:S(2)}) async-start(f32[8,1,4,2,1024]{4,3,2,1,0:T(2,128)} %stack.140), calls=%async_computation | async-start | bytes 524288 | tf_op jit(solution)/shard_map/all_to_all | solution.py:125
  27.6 11.0 %copy-start.1 = (f32[2,32,32,32]{3,2,1,0:T(8,128)}, f32[2,32,32,32]{3,2,1,0:T(8,128)S(1)}, u32[]{:S(2)}) copy-start(f32[2,32,32,32]{3,2,1,0:T(8,128)S(1)} %squeeze.121) | copy-start | bytes 786436
  44.3 9.8 copy-start.21
  46.8 97.4 %collective-permute-start.1 = (f32[1,2,1024]{2,1,0:T(2,128)}, f32[1,2,1024]{2,1,0:T(2,128)}, u32[]{:S(2)}, u32[]{:S(2)}) collective-permute-start(f32[1,2,1024]{2,1,0:T(2,128)} %stack_reshape_squeeze.37), channel_id=1, source_target_pairs={{0,1},{1,2},{2,3},{3,4},{4,5},{5,6},{6,7},{7,8},{8,9},{9,10},{10,1... | collective-permute-start | bytes 24584 | tf_op jit(solution)/shard_map/ppermute | solution.py:19
  51.6 89.0 %collective-permute-start = (f32[1,2,1024]{2,1,0:T(2,128)}, f32[1,2,1024]{2,1,0:T(2,128)}, u32[]{:S(2)}, u32[]{:S(2)}) collective-permute-start(f32[1,2,1024]{2,1,0:T(2,128)} %stack_reshape_squeeze.36), channel_id=1, source_target_pairs={{1,0},{2,1},{3,2},{4,3},{5,4},{6,5},{7,6},{8,7},{9,8},{10,9},{11,1... | collective-permute-start | bytes 24584 | tf_op jit(solution)/shard_map/ppermute | solution.py:22
  63.0 21.3 %copy-start.7 = (f32[2,32,32,32]{3,2,1,0:T(8,128)S(1)}, f32[2,32,32,32]{3,2,1,0:T(8,128)}, u32[]{:S(2)}) copy-start(f32[2,32,32,32]{3,2,1,0:T(8,128)} %copy-done.6) | copy-start | bytes 786436
  84.3 53.7 %copy-start.53 = (f32[2,31,1024]{2,1,0:T(8,128)S(1)}, f32[2,31,1024]{2,1,0:T(8,128)}, u32[]{:S(2)}) copy-start(f32[2,31,1024]{2,1,0:T(8,128)} %get-tuple-element.138) | copy-start | bytes 761860
  86.0 53.3 %copy-start.54 = (f32[2,31,1024]{2,1,0:T(8,128)S(1)}, f32[2,31,1024]{2,1,0:T(8,128)}, u32[]{:S(2)}) copy-start(f32[2,31,1024]{2,1,0:T(8,128)} %get-tuple-element.139) | copy-start | bytes 761860
  189.7 69.5 %all-to-all-start.1 = ((f32[8,1,4,2,1024]{4,3,2,1,0:T(2,128)}), f32[8,1,4,2,1024]{4,3,2,1,0:T(2,128)}, u32[]{:S(2)}, u32[]{:S(2)}) async-start(f32[8,1,4,2,1024]{4,3,2,1,0:T(2,128)} %stack.147), calls=%async_computation.1 | async-start | bytes 524288 | tf_op jit(solution)/shard_map/all_to_all | solution.py:125
  210.4 32.2 %collective-permute-start.3 = (f32[1,2,1024]{2,1,0:T(2,128)}, f32[1,2,1024]{2,1,0:T(2,128)}, u32[]{:S(2)}, u32[]{:S(2)}) collective-permute-start(f32[1,2,1024]{2,1,0:T(2,128)} %stack_reshape_squeeze.39), channel_id=1, source_target_pairs={{0,1},{1,2},{2,3},{3,4},{4,5},{5,6},{6,7},{7,8},{8,9},{9,10},{10,1... | collective-permute-start | bytes 24584 | tf_op jit(solution)/shard_map/ppermute | solution.py:19
  212.2 38.7 %collective-permute-start.2 = (f32[1,2,1024]{2,1,0:T(2,128)}, f32[1,2,1024]{2,1,0:T(2,128)}, u32[]{:S(2)}, u32[]{:S(2)}) collective-permute-start(f32[1,2,1024]{2,1,0:T(2,128)} %stack_reshape_squeeze.38), channel_id=1, source_target_pairs={{1,0},{2,1},{3,2},{4,3},{5,4},{6,5},{7,6},{8,7},{9,8},{10,9},{11,1... | collective-permute-start | bytes 24584 | tf_op jit(solution)/shard_map/ppermute | solution.py:22
  410.2 58.2 %all-to-all-start.2 = ((f32[8,1,4,2,1024]{4,3,2,1,0:T(2,128)}), f32[8,1,4,2,1024]{4,3,2,1,0:T(2,128)}, u32[]{:S(2)}, u32[]{:S(2)}) async-start(f32[8,1,4,2,1024]{4,3,2,1,0:T(2,128)} %stack.153), calls=%async_computation.2 | async-start | bytes 524288 | tf_op jit(solution)/shard_map/all_to_all | solution.py:125
  424.9 26.9 %collective-permute-start.5 = (f32[1,2,1024]{2,1,0:T(2,128)}, f32[1,2,1024]{2,1,0:T(2,128)}, u32[]{:S(2)}, u32[]{:S(2)}) collective-permute-start(f32[1,2,1024]{2,1,0:T(2,128)} %stack_reshape_squeeze.41), channel_id=1, source_target_pairs={{0,1},{1,2},{2,3},{3,4},{4,5},{5,6},{6,7},{7,8},{8,9},{9,10},{10,1... | collective-permute-start | bytes 24584 | tf_op jit(solution)/shard_map/ppermute | solution.py:19
  426.8 33.3 %collective-permute-start.4 = (f32[1,2,1024]{2,1,0:T(2,128)}, f32[1,2,1024]{2,1,0:T(2,128)}, u32[]{:S(2)}, u32[]{:S(2)}) collective-permute-start(f32[1,2,1024]{2,1,0:T(2,128)} %stack_reshape_squeeze.40), channel_id=1, source_target_pairs={{1,0},{2,1},{3,2},{4,3},{5,4},{6,5},{7,6},{8,7},{9,8},{10,9},{11,1... | collective-permute-start | bytes 24584 | tf_op jit(solution)/shard_map/ppermute | solution.py:22
  567.2 16.4 %copy-start.8 = (f32[2,32,32,31]{3,2,1,0:T(8,128)}, f32[2,32,32,31]{3,2,1,0:T(8,128)S(1)}, u32[]{:S(2)}) copy-start(f32[2,32,32,31]{3,2,1,0:T(8,128)S(1)} %get-tuple-element.88) | copy-start | bytes 761860
  571.3 41.1 %all-to-all-start.3 = ((f32[8,1,4,2,1024]{4,3,2,1,0:T(2,128)}), f32[8,1,4,2,1024]{4,3,2,1,0:T(2,128)}, u32[]{:S(2)}, u32[]{:S(2)}) async-start(f32[8,1,4,2,1024]{4,3,2,1,0:T(2,128)} %stack.159), calls=%async_computation.3 | async-start | bytes 524288 | tf_op jit(solution)/shard_map/all_to_all | solution.py:125
  577.2 24.0 %collective-permute-start.7 = (f32[1,2,1024]{2,1,0:T(2,128)}, f32[1,2,1024]{2,1,0:T(2,128)}, u32[]{:S(2)}, u32[]{:S(2)}) collective-permute-start(f32[1,2,1024]{2,1,0:T(2,128)} %stack_reshape_squeeze.43), channel_id=1, source_target_pairs={{0,1},{1,2},{2,3},{3,4},{4,5},{5,6},{6,7},{7,8},{8,9},{9,10},{10,1... | collective-permute-start | bytes 24584 | tf_op jit(solution)/shard_map/ppermute | solution.py:19
  582.0 22.8 %collective-permute-start.6 = (f32[1,2,1024]{2,1,0:T(2,128)}, f32[1,2,1024]{2,1,0:T(2,128)}, u32[]{:S(2)}, u32[]{:S(2)}) collective-permute-start(f32[1,2,1024]{2,1,0:T(2,128)} %stack_reshape_squeeze.42), channel_id=1, source_target_pairs={{1,0},{2,1},{3,2},{4,3},{5,4},{6,5},{7,6},{8,7},{9,8},{10,9},{11,1... | collective-permute-start | bytes 24584 | tf_op jit(solution)/shard_map/ppermute | solution.py:22
  607.5 9.4 copy-start.12
  616.9 70.9 %copy-start.39 = (f32[2,32,1024]{2,1,0:T(8,128)S(1)}, f32[2,32,1024]{2,1,0:T(8,128)}, u32[]{:S(2)}) copy-start(f32[2,32,1024]{2,1,0:T(8,128)} %copy-done.38) | copy-start | bytes 786436
  752.7 56.4 %all-to-all-start.4 = ((f32[8,1,4,2,1024]{4,3,2,1,0:T(2,128)}), f32[8,1,4,2,1024]{4,3,2,1,0:T(2,128)}, u32[]{:S(2)}, u32[]{:S(2)}) async-start(f32[8,1,4,2,1024]{4,3,2,1,0:T(2,128)} %stack.165), calls=%async_computation.4 | async-start | bytes 524288 | tf_op jit(solution)/shard_map/all_to_all | solution.py:125
  767.4 25.1 %collective-permute-start.9 = (f32[1,2,1024]{2,1,0:T(2,128)}, f32[1,2,1024]{2,1,0:T(2,128)}, u32[]{:S(2)}, u32[]{:S(2)}) collective-permute-start(f32[1,2,1024]{2,1,0:T(2,128)} %stack_reshape_squeeze.45), channel_id=1, source_target_pairs={{0,1},{1,2},{2,3},{3,4},{4,5},{5,6},{6,7},{7,8},{8,9},{9,10},{10,1... | collective-permute-start | bytes 24584 | tf_op jit(solution)/shard_map/ppermute | solution.py:19
  769.2 31.5 %collective-permute-start.8 = (f32[1,2,1024]{2,1,0:T(2,128)}, f32[1,2,1024]{2,1,0:T(2,128)}, u32[]{:S(2)}, u32[]{:S(2)}) collective-permute-start(f32[1,2,1024]{2,1,0:T(2,128)} %stack_reshape_squeeze.44), channel_id=1, source_target_pairs={{1,0},{2,1},{3,2},{4,3},{5,4},{6,5},{7,6},{8,7},{9,8},{10,9},{11,1... | collective-permute-start | bytes 24584 | tf_op jit(solution)/shard_map/ppermute | solution.py:22
  804.2 13.8 %copy-start.83 = (f32[2]{0:T(128)S(1)}, f32[2]{0:T(128)}, u32[]{:S(2)}) copy-start(f32[2]{0:T(128)} %copy-done.79) | copy-start | bytes 28
  804.2 13.8 %copy-start.104 = (pred[1024]{0:T(1024)(128)(4,1)S(1)}, pred[1024]{0:T(1024)(128)(4,1)}, u32[]{:S(2)}) copy-start(pred[1024]{0:T(1024)(128)(4,1)} %broadcast_in_dim.679) | copy-start | bytes 3076
  804.2 13.8 %copy-start.106 = (pred[1024]{0:T(1024)(128)(4,1)S(1)}, pred[1024]{0:T(1024)(128)(4,1)}, u32[]{:S(2)}) copy-start(pred[1024]{0:T(1024)(128)(4,1)} %broadcast_in_dim.661) | copy-start | bytes 3076
  804.2 13.8 %copy-start.119 = (f32[2]{0:T(128)S(1)}, f32[2]{0:T(128)}, u32[]{:S(2)}) copy-start(f32[2]{0:T(128)} %copy-done.117) | copy-start | bytes 28
  915.8 33.1 %all-to-all-start.5 = ((f32[8,1,4,2,1024]{4,3,2,1,0:T(2,128)}), f32[8,1,4,2,1024]{4,3,2,1,0:T(2,128)}, u32[]{:S(2)}, u32[]{:S(2)}) async-start(f32[8,1,4,2,1024]{4,3,2,1,0:T(2,128)} %stack.171), calls=%async_computation.5 | async-start | bytes 524288 | tf_op jit(solution)/shard_map/all_to_all | solution.py:125
  920.5 19.2 %collective-permute-start.11 = (f32[1,2,1024]{2,1,0:T(2,128)S(1)}, f32[1,2,1024]{2,1,0:T(2,128)S(1)}, u32[]{:S(2)}, u32[]{:S(2)}) collective-permute-start(f32[1,2,1024]{2,1,0:T(2,128)S(1)} %stack_reshape_squeeze.47), channel_id=1, source_target_pairs={{0,1},{1,2},{2,3},{3,4},{4,5},{5,6},{6,7},{7,8},{8,9},{9,10},{10,1... | collective-permute-start | bytes 24584 | tf_op jit(solution)/shard_map/ppermute | solution.py:19
  924.9 17.6 %collective-permute-start.10 = (f32[1,2,1024]{2,1,0:T(2,128)S(1)}, f32[1,2,1024]{2,1,0:T(2,128)S(1)}, u32[]{:S(2)}, u32[]{:S(2)}) collective-permute-start(f32[1,2,1024]{2,1,0:T(2,128)S(1)} %stack_reshape_squeeze.46), channel_id=1, source_target_pairs={{1,0},{2,1},{3,2},{4,3},{5,4},{6,5},{7,6},{8,7},{9,8},{10,9},{11,1... | collective-permute-start | bytes 24584 | tf_op jit(solution)/shard_map/ppermute | solution.py:22
  943.9 10.1 copy-start.15
  943.9 10.1 copy-start.17
  943.9 10.1 copy-start.19
  944.0 10.1 copy-start.44
  944.0 10.1 copy-start.47
  954.1 70.6 %copy-start.34 = (f32[1,1,2,32,1024]{4,3,2,1,0:T(8,128)S(1)}, f32[1,1,2,32,1024]{4,3,2,1,0:T(8,128)}, u32[]{:S(2)}) copy-start(f32[1,1,2,32,1024]{4,3,2,1,0:T(8,128)} %param.10) | copy-start | bytes 786436
  954.1 70.6 %copy-start.67 = (pred[32,1024]{1,0:T(8,128)(4,1)S(1)}, pred[32,1024]{1,0:T(8,128)(4,1)}, u32[]{:S(2)}) copy-start(pred[32,1024]{1,0:T(8,128)(4,1)} %copy-done.65) | copy-start | bytes 98308
  954.1 70.6 %copy-start.70 = (pred[32,1024]{1,0:T(8,128)(4,1)S(1)}, pred[32,1024]{1,0:T(8,128)(4,1)}, u32[]{:S(2)}) copy-start(pred[32,1024]{1,0:T(8,128)(4,1)} %copy-done.68) | copy-start | bytes 98308
  (132 other events, 491.6 us)
